TPU v7x, 512 devices: a whole 4x4x16 slice. The times are simulated.
512 devices in a mesh: row: 32 (over x, y, core), col: 16 (over z).
Axes of the slice: x: 4, y: 4, z: 16, core: 2. Of those that a mesh axis runs over, the one named last changes fastest.
Arguments:
- tokens: bfloat16 [4096, 2560], P('row', 'col'), may hold values from -6 to 6
- w_gate: bfloat16 [512, 192, 2560], P(('row', 'col')), may hold values from -0.125 to 0.125
- w_up: bfloat16 [512, 192, 2560], P(('row', 'col')), may hold values from -0.125 to 0.125
- w_down: bfloat16 [512, 192, 2560], P(('row', 'col')), may hold values from -0.15625 to 0.15625
- adp_down: bfloat16 [64, 16, 2560], P('row', None, 'col'), may hold values from -0.125 to 0.125
- adp_up: bfloat16 [64, 16, 2560], P('row', None, 'col'), may hold values from -1.5 to 1.5
- expert_ids: int32 [4096, 6], P('row'), may hold values from 0 to 63, all different within a row; in each aligned block of 128 rows (0 to 127, 128 to 255, ...) at most 16 rows name the same one
- gate_vals: float32 [4096, 6], P('row'), may hold values from 0.05 to 0.5
- lengths: int32 [16], replicated, may hold values from 1 to 1365, 4096 in all
- perm: int32 [4096], P('row'), may hold values from 0 to 4095, each once
- req_adapter: int32 [16], replicated, may hold values from 0 to 63
Outputs:
- layer_out: bfloat16 [4096, 2560], P('row', 'col')
Inputs may be any that keep to these rules, and one draw needn't show every extreme that they name: `expert_ids`: within the 128 rows of one index of row, no expert is named by more than 16 rows, a bound that some block reaches; each row names 6 different experts. `perm`: each position appears once. `lengths`: they sum to 4096; the longest is exactly 4096 // 3.
All inputs are finite; a program needn't handle non-finite values.
Results may differ from a plain program's by a relative error of at most 0.0051.
Values may be sent and summed in bfloat16 or wider, within the bound.
A program may use at most 128 MiB of HBM per device.

v0:
```python
import jax
import jax.numpy as jnp
from jax import lax
from jax.sharding import PartitionSpec as P

adapter_scale_factor = 2.0


def contract_last(left, right):
    return lax.dot_general(
        left, right, (((1,), (1,)), ((), ())), preferred_element_type=jnp.float32
    )


def body(
    tokens,
    w_gate,
    w_up,
    w_down,
    adp_down,
    adp_up,
    expert_ids,
    gate_vals,
    lengths,
    perm,
    req_adapter,
):
    count_tok = tokens.shape[0]
    share = tokens.shape[1]
    rows_count = lax.axis_size("row")
    cols_count = lax.axis_size("col")
    experts = 2 * rows_count
    parts = cols_count // 2
    which = lax.axis_index("col") // parts
    topk = expert_ids.shape[1]
    capacity = max(2, (4 * count_tok * topk + 3 * experts - 1) // (3 * experts))
    weight_gate = w_gate[0]
    weight_up = w_up[0]
    down_projection_weight = w_down[0]
    flat_ids = expert_ids.reshape(-1)
    onehot = (flat_ids[:, None] == jnp.arange(experts, dtype=jnp.int32)[None, :]).astype(jnp.int32)
    slot = jnp.sum(onehot * jnp.cumsum(onehot, axis=0), axis=1) - 1
    place = (flat_ids * capacity + slot).reshape(count_tok, topk)
    targets = jnp.arange(experts * capacity, dtype=jnp.int32)
    dispatch = jnp.any(targets[:, None, None] == place[None, :, :], axis=2).astype(jnp.bfloat16)
    combine = jnp.sum(
        jnp.where(
            place[:, :, None] == targets[None, None, :], gate_vals[:, :, None], jnp.float32(0.0)
        ),
        axis=1,
    )
    outgoing = jnp.dot(dispatch, tokens, preferred_element_type=jnp.float32).astype(jnp.bfloat16)
    outgoing = outgoing.reshape(rows_count, 2, capacity, share)
    arrival_rows = lax.all_to_all(outgoing, "row", split_axis=0, concat_axis=0, tiled=True)
    piece = lax.all_gather(arrival_rows, "col", axis=3, tiled=True)
    cols = piece.shape[3]
    mine = lax.dynamic_index_in_dim(piece, which, 1, keepdims=False).reshape(
        rows_count * capacity, cols
    )
    gate = contract_last(mine, weight_gate)
    upper = contract_last(mine, weight_up)
    hidden = (jax.nn.silu(gate) * upper).astype(jnp.bfloat16)
    partial_out = jnp.dot(
        hidden, down_projection_weight, preferred_element_type=jnp.float32
    ).astype(jnp.bfloat16)
    pieces = partial_out.reshape(rows_count * capacity, cols_count, share)
    received = lax.all_to_all(pieces, "col", split_axis=1, concat_axis=1, tiled=True)
    summed = jnp.sum(
        received.astype(jnp.float32).reshape(rows_count, capacity, 2, parts, share), axis=3
    )
    summed = summed.transpose(0, 2, 1, 3)
    returned = lax.all_to_all(summed, "row", split_axis=0, concat_axis=0, tiled=True)
    dispatched_tokens = jnp.dot(
        combine, returned.reshape(experts * capacity, share), precision=lax.Precision.HIGHEST
    )
    down_all, up_all = (
        lax.all_gather(adp_down, "row", axis=0, tiled=True),
        lax.all_gather(adp_up, "row", axis=0, tiled=True),
    )
    adapters = down_all.shape[0]
    rank = down_all.shape[1]
    nreq = lengths.shape[0]
    ends = jnp.cumsum(lengths)
    request = jnp.sum((perm[:, None] >= ends[None, :]).astype(jnp.int32), axis=1)
    adapter = jnp.sum(
        jnp.where(
            request[:, None] == jnp.arange(nreq, dtype=jnp.int32)[None, :], req_adapter[None, :], 0
        ),
        axis=1,
    )
    onehot_a = (adapter[:, None] == jnp.arange(adapters, dtype=jnp.int32)[None, :]).astype(
        jnp.float32
    )
    projected = jnp.einsum(
        "td,kd->tk",
        tokens,
        down_all.reshape(adapters * rank, share),
        preferred_element_type=jnp.float32,
    )
    partial_low = jnp.sum(
        projected.reshape(count_tok, adapters, rank) * onehot_a[:, :, None], axis=1
    )
    low = lax.psum(partial_low, "col").astype(jnp.bfloat16)
    expanded = (onehot_a.astype(jnp.bfloat16)[:, :, None] * low[:, None, :]).reshape(
        count_tok, adapters * rank
    )
    adapter_update = jnp.dot(
        expanded, up_all.reshape(adapters * rank, share), preferred_element_type=jnp.float32
    )
    return (dispatched_tokens + adapter_scale_factor * adapter_update).astype(jnp.bfloat16)


def solution(mesh):
    in_specs = (
        P("row", "col"),
        P(("row", "col"), None, None),
        P(("row", "col"), None, None),
        P(("row", "col"), None, None),
        P("row", None, "col"),
        P("row", None, "col"),
        P("row", None),
        P("row", None),
        P(),
        P("row"),
        P(),
    )
    out_specs = P("row", "col")
    return jax.shard_map(body, mesh=mesh, in_specs=in_specs, out_specs=out_specs, check_vma=False)
```

profile of v0, /device:TPU:1, one launch (start us, length us, event | category | flops | bytes accessed | tf_op | source)
XLA Modules:
  0.0 505.6 jit_solution(4456110021463680649)
XLA Ops:
  6.5 0.9 copy.72
  7.7 1.8 reduce-window.18
  10.2 0.7 multiply_add_fusion
  10.9 0.5 fusion
  11.4 1.0 convolution_convert_fusion.1
  12.6 21.3 %all_to_all.15 = bf16[32,2,16,160]{3,2,1,0:T(8,128)(2,1)S(1)} all-to-all(bf16[32,2,16,160]{3,2,1,0:T(8,128)(2,1)S(1)} %bitcast.59), channel_id=1, replica_groups=mesh['row'=32,'col'=16] {'row'}, dimensions={0} | all-to-all | bytes 655360 | tf_op jit(solution)/shard_map/all_to_all | solution.py:54
  33.9 2.3 copy.77
  36.2 231.6 %all-gather.2.cloned.1.call-done = bf16[32,2,16,2560]{0,2,1,3:T(8,128)(2,1)} async-done(((bf16[32,2,16,160]{0,2,1,3:T(8,128)(2,1)}), bf16[32,2,16,2560]{0,2,1,3:T(8,128)(2,1)}) %all-gather.2.cloned.1.call-update) | async-done | bytes 5242896 | tf_op jit(solution)/shard_map/all_gather | solution.py:55
  267.8 10.4 %constant_dynamic-slice_fusion = bf16[32,1,16,2560]{0,2,1,3:T(8,128)(2,1)} fusion(bf16[32,2,16,2560]{0,2,1,3:T(8,128)(2,1)} %all-gather.2.cloned.1.call-done, s32[]{:T(128)S(6)} %select_n.19), kind=kLoop, calls=%fused_computation.47 | loop fusion | bytes 5242884 | tf_op jit(solution)/shard_map/jit(dynamic_index_in_dim)/dynamic_slice | solution.py:57
  278.2 13.0 %copy.86 = bf16[32,1,16,2560]{3,2,0,1:T(8,128)(2,1)} copy(bf16[32,1,16,2560]{0,2,1,3:T(8,128)(2,1)} %constant_dynamic-slice_fusion) | data formatting | bytes 5242880
  291.2 2.8 fusion.9
  294.1 5.2 %convolution_convert_fusion = bf16[512,2560]{1,0:T(8,128)(2,1)} fusion(bf16[512,2560]{1,0:T(8,128)(2,1)} %bitcast.58, bf16[1,192,2560]{2,1,0:T(8,128)(2,1)S(1)} %copy-done, bf16[1,192,2560]{2,1,0:T(8,128)(2,1)S(1)} %copy-done.7, f32[512,192]{0,1:T(8,128)S(1)} %fusion.9), kind=kOutput, calls=%fused_computation.1 | convolution fusion | flops 1008533504 | bytes 7602176 | tf_op jit(solution)/shard_map/dot_general | solution.py:63
  299.2 4.4 copy.79
  303.6 8.8 %all-to-all-start.1 = ((bf16[512,16,160]{0,2,1:T(8,128)(2,1)}), bf16[512,16,160]{0,2,1:T(8,128)(2,1)}, u32[]{:S(2)}, u32[]{:S(2)}) async-start(bf16[512,16,160]{0,2,1:T(8,128)(2,1)} %bitcast.55), calls=%async_computation.1 | async-start | bytes 5242880 | tf_op jit(solution)/shard_map/all_to_all | solution.py:67
  312.7 25.6 %all_gather.10 = bf16[64,16,160]{2,1,0:T(8,128)(2,1)S(1)} all-gather(bf16[2,16,160]{2,1,0:T(8,128)(2,1)S(1)} %copy-done.2), channel_id=1, replica_groups=mesh['row'=32,'col'=16] {'row'}, dimensions={0}, use_global_device_ids=true | all-gather | bytes 337920 | tf_op jit(solution)/shard_map/all_gather | solution.py:77
  338.4 88.4 %all-to-all-done.1 = bf16[512,16,160]{0,2,1:T(8,128)(2,1)} async-done(((bf16[512,16,160]{0,2,1:T(8,128)(2,1)}), bf16[512,16,160]{0,2,1:T(8,128)(2,1)}, u32[]{:S(2)}, u32[]{:S(2)}) %all-to-all-start.1) | async-done | bytes 2621472 | tf_op jit(solution)/shard_map/all_to_all | solution.py:67
  426.8 2.2 convert_reduce_fusion
  429.0 1.3 copy.85
  430.3 11.3 %all-to-all-start.2 = ((f32[32,2,16,160]{3,1,2,0:T(2,128)}), f32[32,2,16,160]{3,1,2,0:T(2,128)S(1)}, u32[]{:S(2)}, u32[]{:S(2)}) async-start(f32[32,2,16,160]{3,1,2,0:T(2,128)} %bitcast.10), calls=%async_computation.2 | async-start | bytes 2097152 | tf_op jit(solution)/shard_map/all_to_all | solution.py:72
  441.9 22.3 %psum.7 = bf16[128,16]{0,1:T(8,128)(2,1)S(1)} all-reduce(f32[128,16]{0,1:T(8,128)S(1)} %fusion.2), channel_id=1, replica_groups=mesh['row'=32,'col'=16] {'col'}, use_global_device_ids=true, to_apply=%region_10.11 | all-reduce | flops 2048 | bytes 12288 | tf_op jit(solution)/shard_map/psum | solution.py:103
  464.2 31.2 %all_gather.11 = bf16[64,16,160]{2,1,0:T(8,128)(2,1)S(1)} all-gather(bf16[2,16,160]{2,1,0:T(8,128)(2,1)S(1)} %copy-done.3), channel_id=1, replica_groups=mesh['row'=32,'col'=16] {'row'}, dimensions={0}, use_global_device_ids=true | all-gather | bytes 337920 | tf_op jit(solution)/shard_map/all_gather | solution.py:78
  495.5 0.4 select_reduce_fusion
  496.0 1.8 fusion.29
  497.8 1.0 fusion.5
  (41 shorter events, 2.0 us)
Async XLA Ops:
  6.5 287.5 %copy-start = (bf16[1,192,2560]{2,1,0:T(8,128)(2,1)S(1)}, bf16[1,192,2560]{2,1,0:T(8,128)(2,1)}, u32[]{:S(2)}) copy-start(bf16[1,192,2560]{2,1,0:T(8,128)(2,1)} %param.14) | copy-start | bytes 2949124
  6.5 261.2 %all-gather.2.cloned.1.call-start = ((), (), s32[]{:S(2)}) async-start(), calls=%async_computation.3 | async-start | bytes 22282240 | tf_op jit(solution)/shard_map/all_gather | solution.py:55
  278.2 13.1 %copy-start.6 = (bf16[1,192,2560]{2,1,0:T(8,128)(2,1)S(1)}, bf16[1,192,2560]{2,1,0:T(8,128)(2,1)}, u32[]{:S(2)}) copy-start(bf16[1,192,2560]{2,1,0:T(8,128)(2,1)} %param.12) | copy-start | bytes 2949124
  291.2 2.8 copy-start.7
  303.6 8.8 %copy-start.5 = (s32[16]{0:T(128)S(1)}, s32[16]{0:T(128)}, u32[]{:S(2)}) copy-start(s32[16]{0:T(128)} %param.19) | copy-start | bytes 196
  303.6 9.0 %copy-start.2 = (bf16[2,16,160]{2,1,0:T(8,128)(2,1)S(1)}, bf16[2,16,160]{2,1,0:T(8,128)(2,1)}, u32[]{:S(2)}) copy-start(bf16[2,16,160]{2,1,0:T(8,128)(2,1)} %param.15) | copy-start | bytes 30724
  303.6 34.6 %copy-start.8 = (s32[128]{0:T(128)S(1)}, s32[128]{0:T(128)}, u32[]{:S(2)}) copy-start(s32[128]{0:T(128)} %param.20) | copy-start | bytes 1540
  303.6 34.7 %copy-start.9 = (s32[16]{0:T(128)S(1)}, s32[16]{0:T(128)}, u32[]{:S(2)}) copy-start(s32[16]{0:T(128)} %param.21) | copy-start | bytes 196
  303.6 123.2 %all-to-all-start.1 = ((bf16[512,16,160]{0,2,1:T(8,128)(2,1)}), bf16[512,16,160]{0,2,1:T(8,128)(2,1)}, u32[]{:S(2)}, u32[]{:S(2)}) async-start(bf16[512,16,160]{0,2,1:T(8,128)(2,1)} %bitcast.55), calls=%async_computation.1 | async-start | bytes 5242880 | tf_op jit(solution)/shard_map/all_to_all | solution.py:67
  428.9 12.6 %copy-start.1 = (bf16[128,160]{0,1:T(8,128)(2,1)S(1)}, bf16[128,160]{0,1:T(8,128)(2,1)}, u32[]{:S(2)}) copy-start(bf16[128,160]{0,1:T(8,128)(2,1)} %param.11) | copy-start | bytes 122884
  429.0 35.3 %copy-start.3 = (bf16[2,16,160]{2,1,0:T(8,128)(2,1)S(1)}, bf16[2,16,160]{2,1,0:T(8,128)(2,1)}, u32[]{:S(2)}) copy-start(bf16[2,16,160]{2,1,0:T(8,128)(2,1)} %param.16) | copy-start | bytes 30724
  429.0 66.5 %copy-start.4 = (f32[128,6]{0,1:T(8,128)S(1)}, f32[128,6]{0,1:T(8,128)}, u32[]{:S(2)}) copy-start(f32[128,6]{0,1:T(8,128)} %param.18) | copy-start | bytes 9220
  430.3 65.6 %all-to-all-start.2 = ((f32[32,2,16,160]{3,1,2,0:T(2,128)}), f32[32,2,16,160]{3,1,2,0:T(2,128)S(1)}, u32[]{:S(2)}, u32[]{:S(2)}) async-start(f32[32,2,16,160]{3,1,2,0:T(2,128)} %bitcast.10), calls=%async_computation.2 | async-start | bytes 2097152 | tf_op jit(solution)/shard_map/all_to_all | solution.py:72
Sparse Core Ops, SparseCore 0:
  36.3 231.4 all-gather.1
where the time goes:
time: 507 us; the launch traced here: 506 us
  waiting for transfers between devices  320 us (63%)
  blocking collectives  100 us (20%)
  local copies, waits for them, and re-layouts  33.4 us (7%)
  starting transfers between devices  20 us (4%)
  between operations  13.6 us (3%)
  matrix products  12.1 us (2%)
  other arithmetic  6.11 us (1%)
    all_gather x1, waiting for transfers between devices, body(): piece = lax.all_gather(arrival_rows, 'col', axis=3, tiled=True)  232 us
    all_to_all x1, waiting for transfers between devices, body(): lax.all_to_all(pieces, 'col', split_axis=1, concat_axis=1, tiled=True)  88.4 us
    all_gather x1, blocking collectives, body(): lax.all_gather(adp_up, 'row', axis=0, tiled=True)  31.2 us
    all_gather x1, blocking collectives, body(): lax.all_gather(adp_down, 'row', axis=0, tiled=True)  25.6 us
    psum x1, blocking collectives, body(): low = lax.psum(partial_low, 'col').astype(jnp.bfloat16)  22.3 us
    all_to_all x1, blocking collectives, body(): lax.all_to_all(outgoing, 'row', split_axis=0, concat_axis=0, tiled=True)  21.3 us
    unnamed x23, local copies, waits for them, and re-layouts  15.3 us
    all_to_all x1, starting transfers between devices, body(): lax.all_to_all(summed, 'row', split_axis=0, concat_axis=0, tiled=True)  11.3 us
  transfers between devices with their start and end apart: 3, of which 2 were waited for; matrix products, arithmetic and copies ran while one was open for 0% of the time, Pallas kernels for 0%

commit v1 on v0

--- a/solution.py
+++ b/solution.py
@@ -2,6 +2,7 @@
 import jax.numpy as jnp
 from jax import lax
 from jax.sharding import PartitionSpec as P
+from jax.lax import all_gather
 
 adapter_scale_factor = 2.0
 
@@ -100,7 +101,11 @@
     partial_low = jnp.sum(
         projected.reshape(count_tok, adapters, rank) * onehot_a[:, :, None], axis=1
     )
-    low = lax.psum(partial_low, "col").astype(jnp.bfloat16)
+
+    def recover_the_zones(inner_x, across):
+        return all_gather(inner_x, axis_name=across).sum(axis=0)
+
+    low = recover_the_zones(partial_low, "col").astype(jnp.bfloat16)
     expanded = (onehot_a.astype(jnp.bfloat16)[:, :, None] * low[:, None, :]).reshape(
         count_tok, adapters * rank
     )

time: 507 us -> 537 us (1.059)
  waiting for transfers between devices: 320 us -> 346 us
    all_to_all x1, waiting for transfers between devices: 88.4 us -> 114 us  [body(): lax.all_to_all(pieces, 'col', split_axis=1, concat_axis=1, tiled=True)]
    psum x1 -> x0, blocking collectives: 22.3 us -> none  [body(): low = lax.psum(partial_low, 'col').astype(jnp.bfloat16)]
    all_gather x0 -> x1, blocking collectives: none -> 20.5 us  [recover_the_zones(): return all_gather(inner_x, axis_name=across).sum(axis=0)]
    all_gather x1, blocking collectives: 25.6 us -> 33.4 us  [body(): lax.all_gather(adp_down, 'row', axis=0, tiled=True)]
    unnamed x23 -> x24, local copies, waits for them, and re-layouts: 15.3 us -> 15.3 us
where the time goes in v1:
time: 537 us; the launch traced here: 536 us
  waiting for transfers between devices  346 us (64%)
  blocking collectives  105 us (20%)
  local copies, waits for them, and re-layouts  33.5 us (6%)
  starting transfers between devices  20.2 us (4%)
  between operations  13.6 us (3%)
  matrix products  12.1 us (2%)
  other arithmetic  6.14 us (1%)
    all_gather x1, waiting for transfers between devices, body(): piece = lax.all_gather(arrival_rows, 'col', axis=3, tiled=True)  232 us
    all_to_all x1, waiting for transfers between devices, body(): lax.all_to_all(pieces, 'col', split_axis=1, concat_axis=1, tiled=True)  114 us
    all_gather x1, blocking collectives, body(): lax.all_gather(adp_down, 'row', axis=0, tiled=True)  33.4 us
    all_gather x1, blocking collectives, body(): lax.all_gather(adp_up, 'row', axis=0, tiled=True)  29.9 us
    all_to_all x1, blocking collectives, body(): lax.all_to_all(outgoing, 'row', split_axis=0, concat_axis=0, tiled=True)  21.3 us
    all_gather x1, blocking collectives, recover_the_zones(): return all_gather(inner_x, axis_name=across).sum(axis=0)  20.5 us
    unnamed x24, local copies, waits for them, and re-layouts  15.3 us
    all_to_all x1, starting transfers between devices, body(): lax.all_to_all(summed, 'row', split_axis=0, concat_axis=0, tiled=True)  11.4 us
  transfers between devices with their start and end apart: 3, of which 2 were waited for; matrix products, arithmetic and copies ran while one was open for 0% of the time, Pallas kernels for 0%

profile of v1, /device:TPU:1, one launch (start us, length us, event | category | flops | bytes accessed | tf_op | source)
XLA Modules:
  0.0 536.1 jit_solution(4074852227479328554)
XLA Ops:
  6.5 0.9 copy.72
  7.7 1.8 reduce-window.18
  10.2 0.7 multiply_add_fusion
  10.9 0.5 fusion
  11.4 1.0 convolution_convert_fusion.1
  12.6 21.3 %all_to_all.15 = bf16[32,2,16,160]{3,2,1,0:T(8,128)(2,1)S(1)} all-to-all(bf16[32,2,16,160]{3,2,1,0:T(8,128)(2,1)S(1)} %bitcast.64), channel_id=1, replica_groups=mesh['row'=32,'col'=16] {'row'}, dimensions={0} | all-to-all | bytes 655360 | tf_op jit(solution)/shard_map/all_to_all | solution.py:55
  33.9 2.3 copy.77
  36.2 231.6 %all-gather.3.cloned.1.call-done = bf16[32,2,16,2560]{0,2,1,3:T(8,128)(2,1)} async-done(((bf16[32,2,16,160]{0,2,1,3:T(8,128)(2,1)}), bf16[32,2,16,2560]{0,2,1,3:T(8,128)(2,1)}) %all-gather.3.cloned.1.call-update) | async-done | bytes 5242896 | tf_op jit(solution)/shard_map/all_gather | solution.py:56
  267.8 10.4 %constant_dynamic-slice_fusion = bf16[32,1,16,2560]{0,2,1,3:T(8,128)(2,1)} fusion(bf16[32,2,16,2560]{0,2,1,3:T(8,128)(2,1)} %all-gather.3.cloned.1.call-done, s32[]{:T(128)S(6)} %select_n.19), kind=kLoop, calls=%fused_computation.48 | loop fusion | bytes 5242884 | tf_op jit(solution)/shard_map/jit(dynamic_index_in_dim)/dynamic_slice | solution.py:58
  278.2 13.0 %copy.86 = bf16[32,1,16,2560]{3,2,0,1:T(8,128)(2,1)} copy(bf16[32,1,16,2560]{0,2,1,3:T(8,128)(2,1)} %constant_dynamic-slice_fusion) | data formatting | bytes 5242880
  291.2 2.8 fusion.9
  294.1 5.2 convolution_convert_fusion
  299.2 4.4 copy.79
  303.6 8.8 %all-to-all-start.1 = ((bf16[512,16,160]{0,2,1:T(8,128)(2,1)}), bf16[512,16,160]{0,2,1:T(8,128)(2,1)}, u32[]{:S(2)}, u32[]{:S(2)}) async-start(bf16[512,16,160]{0,2,1:T(8,128)(2,1)} %bitcast.60), calls=%async_computation.1 | async-start | bytes 5242880 | tf_op jit(solution)/shard_map/all_to_all | solution.py:68
  312.8 113.9 %all-to-all-done.1 = bf16[512,16,160]{0,2,1:T(8,128)(2,1)} async-done(((bf16[512,16,160]{0,2,1:T(8,128)(2,1)}), bf16[512,16,160]{0,2,1:T(8,128)(2,1)}, u32[]{:S(2)}, u32[]{:S(2)}) %all-to-all-start.1) | async-done | bytes 2621472 | tf_op jit(solution)/shard_map/all_to_all | solution.py:68
  426.8 2.2 convert_reduce_fusion
  429.0 1.3 copy.85
  430.3 11.4 %all-to-all-start.2 = ((f32[32,2,16,160]{3,1,2,0:T(2,128)}), f32[32,2,16,160]{3,1,2,0:T(2,128)S(1)}, u32[]{:S(2)}, u32[]{:S(2)}) async-start(f32[32,2,16,160]{3,1,2,0:T(2,128)} %bitcast.10), calls=%async_computation.2 | async-start | bytes 2097152 | tf_op jit(solution)/shard_map/all_to_all | solution.py:73
  441.7 33.4 %all_gather.16 = bf16[64,16,160]{2,1,0:T(8,128)(2,1)S(1)} all-gather(bf16[2,16,160]{2,1,0:T(8,128)(2,1)S(1)} %copy-done.2), channel_id=1, replica_groups=mesh['row'=32,'col'=16] {'row'}, dimensions={0}, use_global_device_ids=true | all-gather | bytes 337920 | tf_op jit(solution)/shard_map/all_gather | solution.py:78
  475.5 20.5 %all-gather = f32[2048,16]{0,1:T(8,128)S(1)} all-gather(f32[128,16]{0,1:T(8,128)S(1)} %fusion.2), channel_id=2, replica_groups=mesh['row'=32,'col'=16] {'col'}, dimensions={0}, use_global_device_ids=true | all-gather | bytes 139264 | tf_op jit(solution)/shard_map/all_gather | solution.py:106
  496.0 29.9 %all_gather.19 = bf16[64,16,160]{2,1,0:T(8,128)(2,1)S(1)} all-gather(bf16[2,16,160]{2,1,0:T(8,128)(2,1)S(1)} %copy-done.3), channel_id=1, replica_groups=mesh['row'=32,'col'=16] {'row'}, dimensions={0}, use_global_device_ids=true | all-gather | bytes 337920 | tf_op jit(solution)/shard_map/all_gather | solution.py:79
  525.9 0.4 select_reduce_fusion
  526.5 1.8 fusion.29
  528.3 1.0 fusion.5
  (43 shorter events, 2.1 us)
Async XLA Ops:
  6.5 287.5 %copy-start = (bf16[1,192,2560]{2,1,0:T(8,128)(2,1)S(1)}, bf16[1,192,2560]{2,1,0:T(8,128)(2,1)}, u32[]{:S(2)}) copy-start(bf16[1,192,2560]{2,1,0:T(8,128)(2,1)} %param.14) | copy-start | bytes 2949124
  6.5 261.2 %all-gather.3.cloned.1.call-start = ((), (), s32[]{:S(2)}) async-start(), calls=%async_computation.3 | async-start | bytes 22282240 | tf_op jit(solution)/shard_map/all_gather | solution.py:56
  278.2 13.1 %copy-start.6 = (bf16[1,192,2560]{2,1,0:T(8,128)(2,1)S(1)}, bf16[1,192,2560]{2,1,0:T(8,128)(2,1)}, u32[]{:S(2)}) copy-start(bf16[1,192,2560]{2,1,0:T(8,128)(2,1)} %param.12) | copy-start | bytes 2949124
  291.2 2.8 copy-start.7
  303.6 8.8 %copy-start.5 = (s32[16]{0:T(128)S(1)}, s32[16]{0:T(128)}, u32[]{:S(2)}) copy-start(s32[16]{0:T(128)} %param.19) | copy-start | bytes 196
  303.6 9.0 %copy-start.8 = (s32[128]{0:T(128)S(1)}, s32[128]{0:T(128)}, u32[]{:S(2)}) copy-start(s32[128]{0:T(128)} %param.20) | copy-start | bytes 1540
  303.6 9.1 %copy-start.9 = (s32[16]{0:T(128)S(1)}, s32[16]{0:T(128)}, u32[]{:S(2)}) copy-start(s32[16]{0:T(128)} %param.21) | copy-start | bytes 196
  303.6 123.2 %all-to-all-start.1 = ((bf16[512,16,160]{0,2,1:T(8,128)(2,1)}), bf16[512,16,160]{0,2,1:T(8,128)(2,1)}, u32[]{:S(2)}, u32[]{:S(2)}) async-start(bf16[512,16,160]{0,2,1:T(8,128)(2,1)} %bitcast.60), calls=%async_computation.1 | async-start | bytes 5242880 | tf_op jit(solution)/shard_map/all_to_all | solution.py:68
  428.9 12.7 %copy-start.2 = (bf16[2,16,160]{2,1,0:T(8,128)(2,1)S(1)}, bf16[2,16,160]{2,1,0:T(8,128)(2,1)}, u32[]{:S(2)}) copy-start(bf16[2,16,160]{2,1,0:T(8,128)(2,1)} %param.15) | copy-start | bytes 30724
  428.9 46.2 %copy-start.1 = (bf16[128,160]{0,1:T(8,128)(2,1)S(1)}, bf16[128,160]{0,1:T(8,128)(2,1)}, u32[]{:S(2)}) copy-start(bf16[128,160]{0,1:T(8,128)(2,1)} %param.11) | copy-start | bytes 122884
  429.0 67.1 %copy-start.3 = (bf16[2,16,160]{2,1,0:T(8,128)(2,1)S(1)}, bf16[2,16,160]{2,1,0:T(8,128)(2,1)}, u32[]{:S(2)}) copy-start(bf16[2,16,160]{2,1,0:T(8,128)(2,1)} %param.16) | copy-start | bytes 30724
  430.3 95.7 %copy-start.4 = (f32[128,6]{0,1:T(8,128)S(1)}, f32[128,6]{0,1:T(8,128)}, u32[]{:S(2)}) copy-start(f32[128,6]{0,1:T(8,128)} %param.18) | copy-start | bytes 9220
  430.3 96.1 %all-to-all-start.2 = ((f32[32,2,16,160]{3,1,2,0:T(2,128)}), f32[32,2,16,160]{3,1,2,0:T(2,128)S(1)}, u32[]{:S(2)}, u32[]{:S(2)}) async-start(f32[32,2,16,160]{3,1,2,0:T(2,128)} %bitcast.10), calls=%async_computation.2 | async-start | bytes 2097152 | tf_op jit(solution)/shard_map/all_to_all | solution.py:73
Sparse Core Ops, SparseCore 0:
  36.3 231.4 all-gather.2
